TPU v7x, 32 devices: a whole 2x2x4 slice. The times are simulated.
32 devices in a mesh: group: 2 (over y), section: 4 (over z), span: 2 (over x), mp: 2 (over core).
Axes of the slice: x: 2, y: 2, z: 4, core: 2. Of those that a mesh axis runs over, the one named last changes fastest.
Arguments:
- queries: bfloat16 [8, 256, 4096], P(('group', 'section'), None, ('span', 'mp')), parts along dimension 0, may hold values from -5 to 5
- keys_values: bfloat16 [2, 8, 256, 4096], P(None, ('group', 'section'), None, ('span', 'mp')), parts along dimension 1, may hold values from -5 to 5
- latents: bfloat16 [8, 256, 5120], P(('group', 'section'), ('span', 'mp')), parts along dimension 0, may hold values from -6 to 6
- out_weight: bfloat16 [4096, 5120], P(('span', 'mp')), may hold values from -3 to 3
- gate_table: float32 [8, 5120], replicated, may hold values from 0.5 to 1.5
- level_index: int32 [8], P(('group', 'section')), parts along dimension 0, may hold values from 0 to 7
- pair_window: int32 [6], P('group'), parts along dimension 0, may hold values from 0 to 256
Outputs:
- shifted: bfloat16 [8, 256, 5120], P(('group', 'section'), ('span', 'mp')), parts along dimension 0
There are 2 independent parts, one for each index of `group`. A program takes and returns all parts, laid end to end along the dimension named above; an argument that names none is the same for every part. Nothing has to cross between parts.
All inputs are finite; a program needn't handle non-finite values.
Results may differ from a plain program's by a relative error of at most 0.015.
Values may be sent and summed in bfloat16 or wider, within the bound.
A program may use at most 64 MiB of HBM per device.

v0:
```python
import math

import jax
import jax.numpy as jnp
from jax import lax
from jax.sharding import PartitionSpec as P

HD = 128


NEG_BIG = -1e30


def extended(array, sides, width):
    for axis, dim in sides:
        size, length = (lax.axis_size(axis), array.shape[dim])
        up = [(i, (i + 1) % size) for i in range(size - 1)]
        down = [(j, i) for i, j in up]
        last = lax.slice_in_dim(array, length - width, length, axis=dim)
        first = lax.slice_in_dim(array, 0, width, axis=dim)
        before = lax.ppermute(last, axis, up)
        after = lax.ppermute(first, axis, down)
        array = jnp.concatenate([before, array, after], axis=dim)
    return array


def from_behind(value, axis, steps):
    count = lax.axis_size(axis)
    pairs = [(source, (source + steps) % count) for source in range(count)]
    return lax.ppermute(value, axis, pairs)


def split_heads(flat_rows):
    return flat_rows.reshape(flat_rows.shape[0], -1, HD)


def block_partial(query_block, key_rows, value_rows, key_mask):
    score_scale = 1.0 / math.sqrt(HD)
    scores = (
        jnp.einsum("bhd,khd->hbk", query_block, key_rows, preferred_element_type=jnp.float32)
        * score_scale
    )
    scores = jnp.where(key_mask[None, None, :], scores, NEG_BIG)
    row_max = jnp.max(scores, axis=-1)
    probabilities = jnp.where(key_mask[None, None, :], jnp.exp(scores - row_max[..., None]), 0.0)
    row_total = jnp.sum(probabilities, axis=-1)
    weighted = jnp.einsum(
        "hbk,khd->bhd",
        probabilities.astype(jnp.bfloat16),
        value_rows,
        preferred_element_type=jnp.float32,
    )
    return (weighted, row_max, row_total)


def shards(queries, keys_values, latents, out_weight, gate_table, level_index, pair_window):
    sections = lax.axis_size("section")
    section_id = lax.axis_index("section")
    span_tok = queries.shape[1]
    width_local = queries.shape[2]
    block_rows = min(512, span_tok)
    blocks = span_tok // block_rows
    final_pair = pair_window.shape[0] - 1
    prev_width = jnp.where(section_id > 0, pair_window[jnp.clip(section_id - 1, 0, final_pair)], 0)
    next_width = jnp.where(
        section_id < sections - 1, pair_window[jnp.clip(section_id, 0, final_pair)], 0
    )
    row_ids = jnp.arange(span_tok, dtype=jnp.int32)
    own_queries = queries[0]
    query_blocks = split_heads(own_queries).reshape(blocks, block_rows, -1, HD)
    ones_mask = jnp.ones((span_tok,), bool)
    padded = extended(keys_values, (("section", 1),), 1)
    key_rows = split_heads(padded[0].reshape(3 * span_tok, width_local))
    value_rows = split_heads(padded[1].reshape(3 * span_tok, width_local))
    key_mask = jnp.concatenate(
        [row_ids >= span_tok - prev_width, ones_mask, row_ids < next_width], 0
    )

    def one_block(query_block):
        weighted, row_max, row_total = block_partial(query_block, key_rows, value_rows, key_mask)
        return (weighted / jnp.swapaxes(row_total, 0, 1)[:, :, None]).astype(jnp.bfloat16)

    attended = lax.map(one_block, query_blocks)
    attended = attended.reshape(span_tok, width_local)
    summed = lax.psum_scatter(
        jnp.dot(attended, out_weight, preferred_element_type=jnp.float32).astype(jnp.bfloat16),
        ("span", "mp"),
        scatter_dimension=0,
        tiled=True,
    ).astype(jnp.float32)
    one_hot = (level_index[0] == jnp.arange(gate_table.shape[0], dtype=jnp.int32)).astype(
        jnp.float32
    )
    gate_row = jnp.sum(one_hot[:, None] * gate_table, axis=0)
    updated = (latents[0].astype(jnp.float32) + gate_row[None, :] * summed).astype(jnp.bfloat16)
    shifted = from_behind(updated, "section", 1)
    return shifted[None]


def solution(mesh):
    in_specs = (
        P(("group", "section"), None, ("span", "mp")),
        P(None, ("group", "section"), None, ("span", "mp")),
        P(("group", "section"), ("span", "mp"), None),
        P(("span", "mp"), None),
        P(),
        P(("group", "section")),
        P("group"),
    )
    out_specs = P(("group", "section"), ("span", "mp"), None)
    return jax.shard_map(shards, mesh=mesh, in_specs=in_specs, out_specs=out_specs, check_vma=False)
```

profile of v0, /device:TPU:0, one launch (start us, length us, event | category | flops | bytes accessed | tf_op | source)
XLA Modules:
  0.0 110.5 jit_solution(15434429009313025589)
XLA Ops:
  6.5 0.0 reduce-scatter.2.cloned.1.call-start
  6.5 6.1 %collective-permute-start = (bf16[2,1,256,1024]{3,2,1,0:T(8,128)(2,1)}, bf16[2,1,256,1024]{3,2,1,0:T(8,128)(2,1)}, u32[]{:S(2)}, u32[]{:S(2)}) collective-permute-start(bf16[2,1,256,1024]{3,2,1,0:T(8,128)(2,1)} %param.8), channel_id=1, source_target_pairs={{0,4},{4,8},{8,12},{1,5},{5,9},{9,13},{2,6},{6,10},{10,14},{3,7},{... | collective-permute-start | bytes 3145736 | tf_op jit(solution)/shard_map/ppermute | solution.py:21
  12.6 1.3 %collective-permute-start.1 = (bf16[2,1,256,1024]{3,2,1,0:T(8,128)(2,1)}, bf16[2,1,256,1024]{3,2,1,0:T(8,128)(2,1)S(1)}, u32[]{:S(2)}, u32[]{:S(2)}) collective-permute-start(bf16[2,1,256,1024]{3,2,1,0:T(8,128)(2,1)} %param.8), channel_id=1, source_target_pairs={{4,0},{8,4},{12,8},{5,1},{9,5},{13,9},{6,2},{10,6},{14,10},{7,3},{... | collective-permute-start | bytes 3145736 | tf_op jit(solution)/shard_map/ppermute | solution.py:22
  13.9 1.1 %copy.18 = bf16[32,8,8,128]{3,2,1,0:T(8,128)(2,1)S(1)} copy(bf16[32,8,8,128]{3,1,2,0:T(8,128)(2,1)} %bitcast.52) | data formatting | bytes 1048576
  15.0 1.4 %fusion.34 = (s32[1]{0:T(128)}, s32[1]{0:T(128)}) fusion(s32[3]{0:T(128)} %param.13, s32[]{:T(128)S(6)} %min.7, s32[]{:T(128)S(6)} %min.8), kind=kLoop, calls=%fused_computation.33 | loop fusion | bytes 24 | tf_op jit(solution)/shard_map/dynamic_slice | solution.py:64
  17.7 16.6 %collective-permute-done = bf16[2,1,256,1024]{3,2,1,0:T(8,128)(2,1)} collective-permute-done((bf16[2,1,256,1024]{3,2,1,0:T(8,128)(2,1)}, bf16[2,1,256,1024]{3,2,1,0:T(8,128)(2,1)}, u32[]{:S(2)}, u32[]{:S(2)}) %collective-permute-start) | collective-permute-done | bytes 1048608 | tf_op jit(solution)/shard_map/ppermute | solution.py:21
  34.3 1.3 %constant_dynamic-update-slice_fusion.2 = bf16[2,3,256,1024]{3,2,1,0:T(8,128)(2,1)S(1)} fusion(bf16[2,1,256,1024]{3,2,1,0:T(8,128)(2,1)} %collective-permute-done), kind=kLoop, calls=%fused_computation.25 | loop fusion | bytes 2097152
  35.6 0.0 copy-done
  35.6 0.1 constant_dynamic-update-slice_fusion.1
  35.7 3.6 %collective-permute-done.1 = bf16[2,1,256,1024]{3,2,1,0:T(8,128)(2,1)S(1)} collective-permute-done((bf16[2,1,256,1024]{3,2,1,0:T(8,128)(2,1)}, bf16[2,1,256,1024]{3,2,1,0:T(8,128)(2,1)S(1)}, u32[]{:S(2)}, u32[]{:S(2)}) %collective-permute-start.1) | collective-permute-done | bytes 1048608 | tf_op jit(solution)/shard_map/ppermute | solution.py:22
  39.3 0.1 constant_dynamic-update-slice_fusion
  39.4 0.6 fusion.33
  40.0 0.4 copy.17
  40.4 0.4 copy.16
  40.9 0.0 slice-start
  40.9 1.0 fusion.12
  41.9 0.0 slice-start.1
  41.9 0.0 slice-start.2
  41.9 2.4 %fusion.35 = (f32[8,256]{1,0:T(8,128)S(1)}, bf16[8,256,768]{1,2,0:T(8,128)(2,1)S(1)}) fusion(f32[8,768,256]{2,1,0:T(8,128)S(1)} %fusion.12, pred[768]{0:T(1024)(128)(4,1)S(1)} %pad_add_fusion), kind=kOutput, calls=%fused_computation.34 | output fusion | flops 12583679 | bytes 9446144 | tf_op jit(solution)/shard_map/while/body/eval_jaxpr/sub | solution.py:45
  44.3 0.7 fusion.25
  45.0 0.0 slice-done
  45.0 0.0 slice-done.1
  45.0 0.1 slice-done.2
  45.2 4.3 %convolution_convert_fusion = bf16[256,5120]{1,0:T(8,128)(2,1)} fusion(bf16[256,1024]{0,1:T(8,128)(2,1)S(1)} %bitcast.50, bf16[1024,5120]{1,0:T(8,128)(2,1)S(1)} %bitcast.44), kind=kOutput, calls=%fused_computation.1 | convolution fusion | flops 2685665280 | bytes 13631488 | tf_op jit(solution)/shard_map/dot_general | solution.py:86
  49.5 0.0 reduce-scatter.2.cloned.1.call-update
  50.2 0.0 copy-done.2
  50.2 0.1 multiply_reduce_fusion
  50.3 33.1 %reduce-scatter.2.cloned.1.call-done = bf16[64,5120]{1,0:T(8,128)(2,1)} async-done(((bf16[256,5120]{1,0:T(8,128)(2,1)}), bf16[64,5120]{1,0:T(8,128)(2,1)}) %reduce-scatter.2.cloned.1.call-update) | async-done | bytes 655376 | tf_op jit(solution)/shard_map/reduce_scatter | solution.py:85
  83.4 1.3 %fusion.19 = bf16[64,5120]{1,0:T(8,128)(2,1)S(1)} fusion(bf16[64,5120]{1,0:T(8,128)(2,1)} %reduce-scatter.2.cloned.1.call-done, bf16[1,64,5120]{2,1,0:T(8,128)(2,1)S(1)} %copy-done.1, f32[5120]{0:T(1024)S(1)} %multiply_reduce_fusion), kind=kLoop, calls=%fused_computation.18 | loop fusion | flops 1638400 | bytes 1986560 | tf_op jit(solution)/shard_map/convert_element_type | solution.py:95
  84.7 1.5 %collective-permute-start.2 = (bf16[64,5120]{1,0:T(8,128)(2,1)S(1)}, bf16[64,5120]{1,0:T(8,128)(2,1)S(1)}, u32[]{:S(2)}, u32[]{:S(2)}) collective-permute-start(bf16[64,5120]{1,0:T(8,128)(2,1)S(1)} %fusion.19), channel_id=1, source_target_pairs={{0,4},{4,8},{8,12},{12,0},{1,5},{5,9},{9,13},{13,1},{2,6},{6,10},{... | collective-permute-start | bytes 1966088 | tf_op jit(solution)/shard_map/ppermute | solution.py:30
  86.2 16.6 %collective-permute-done.2 = bf16[64,5120]{1,0:T(8,128)(2,1)S(1)} collective-permute-done((bf16[64,5120]{1,0:T(8,128)(2,1)S(1)}, bf16[64,5120]{1,0:T(8,128)(2,1)S(1)}, u32[]{:S(2)}, u32[]{:S(2)}) %collective-permute-start.2) | collective-permute-done | bytes 655392 | tf_op jit(solution)/shard_map/ppermute | solution.py:30
  102.9 0.8 copy.35
  (9 shorter events, 0.0 us)
Async XLA Ops:
  6.5 29.1 %copy-start = (bf16[2,1,256,1024]{3,2,1,0:T(8,128)(2,1)S(1)}, bf16[2,1,256,1024]{3,2,1,0:T(8,128)(2,1)}, u32[]{:S(2)}) copy-start(bf16[2,1,256,1024]{3,2,1,0:T(8,128)(2,1)} %param.8) | copy-start | bytes 3145732
  6.5 76.9 %reduce-scatter.2.cloned.1.call-start = ((), (), s32[]{:S(2)}) async-start(), calls=%async_computation.1 | async-start | bytes 3276800 | tf_op jit(solution)/shard_map/reduce_scatter | solution.py:85
  6.5 27.8 %collective-permute-start = (bf16[2,1,256,1024]{3,2,1,0:T(8,128)(2,1)}, bf16[2,1,256,1024]{3,2,1,0:T(8,128)(2,1)}, u32[]{:S(2)}, u32[]{:S(2)}) collective-permute-start(bf16[2,1,256,1024]{3,2,1,0:T(8,128)(2,1)} %param.8), channel_id=1, source_target_pairs={{0,4},{4,8},{8,12},{1,5},{5,9},{9,13},{2,6},{6,10},{10,14},{3,7},{... | collective-permute-start | bytes 3145736 | tf_op jit(solution)/shard_map/ppermute | solution.py:21
  12.6 26.7 %collective-permute-start.1 = (bf16[2,1,256,1024]{3,2,1,0:T(8,128)(2,1)}, bf16[2,1,256,1024]{3,2,1,0:T(8,128)(2,1)S(1)}, u32[]{:S(2)}, u32[]{:S(2)}) collective-permute-start(bf16[2,1,256,1024]{3,2,1,0:T(8,128)(2,1)} %param.8), channel_id=1, source_target_pairs={{4,0},{8,4},{12,8},{5,1},{9,5},{13,9},{6,2},{10,6},{14,10},{7,3},{... | collective-permute-start | bytes 3145736 | tf_op jit(solution)/shard_map/ppermute | solution.py:22
  40.9 4.1 %slice-start = ((s8[10485760]{0:T(1024)(128)(4,1)}), s8[4194304]{0:T(1024)(128)(4,1)S(1)}, s32[]{:S(2)}) async-start(s8[10485760]{0:T(1024)(128)(4,1)} %bitcast.43), calls=%async_computation.2 | async-start | bytes 8388608
  41.9 3.2 %slice-start.1 = ((s8[10485760]{0:T(1024)(128)(4,1)}), s8[4194304]{0:T(1024)(128)(4,1)S(1)}, s32[]{:S(2)}) async-start(s8[10485760]{0:T(1024)(128)(4,1)} %bitcast.43), calls=%async_computation.3 | async-start | bytes 8388608
  41.9 3.3 %slice-start.2 = ((s8[10485760]{0:T(1024)(128)(4,1)}), s8[2097152]{0:T(1024)(128)(4,1)S(1)}, s32[]{:S(2)}) async-start(s8[10485760]{0:T(1024)(128)(4,1)} %bitcast.43), calls=%async_computation.4 | async-start | bytes 4194304
  45.2 5.0 %copy-start.2 = (f32[8,5120]{1,0:T(8,128)S(1)}, f32[8,5120]{1,0:T(8,128)}, u32[]{:S(2)}) copy-start(f32[8,5120]{1,0:T(8,128)} %param.11) | copy-start | bytes 491524
  49.5 34.0 %copy-start.1 = (bf16[1,64,5120]{2,1,0:T(8,128)(2,1)S(1)}, bf16[1,64,5120]{2,1,0:T(8,128)(2,1)}, u32[]{:S(2)}) copy-start(bf16[1,64,5120]{2,1,0:T(8,128)(2,1)} %param.9) | copy-start | bytes 1966084
  84.7 18.2 %collective-permute-start.2 = (bf16[64,5120]{1,0:T(8,128)(2,1)S(1)}, bf16[64,5120]{1,0:T(8,128)(2,1)S(1)}, u32[]{:S(2)}, u32[]{:S(2)}) collective-permute-start(bf16[64,5120]{1,0:T(8,128)(2,1)S(1)} %fusion.19), channel_id=1, source_target_pairs={{0,4},{4,8},{8,12},{12,0},{1,5},{5,9},{9,13},{13,1},{2,6},{6,10},{... | collective-permute-start | bytes 1966088 | tf_op jit(solution)/shard_map/ppermute | solution.py:30
Sparse Core Ops, SparseCore 0:
  49.6 33.7 reduce-scatter.1
where the time goes:
time: 111 us
  waiting for transfers between devices  69.9 us (63%)
  between operations  15.5 us (14%)
  starting transfers between devices  8.88 us (8%)
  local copies, waits for them, and re-layouts  6.43 us (6%)
  matrix products  5.96 us (5%)
  other arithmetic  3.82 us (3%)
    reduce_scatter x1, waiting for transfers between devices, shards(): lax.psum_scatter(jnp.dot(attended, out_weight, preferred_element_type=jnp...  33.1 us
    ppermute x1, waiting for transfers between devices, from_behind(): return lax.ppermute(value, axis, pairs)  16.6 us
    ppermute x1, waiting for transfers between devices, extended(): before = lax.ppermute(last, axis, up)  16.6 us
    ppermute x1, starting transfers between devices, extended(): before = lax.ppermute(last, axis, up)  6.05 us
    unnamed x18, local copies, waits for them, and re-layouts  4.4 us
    dot_general x1, matrix products, shards(): jnp.dot(attended, out_weight, preferred_element_type=jnp.float32)  4.28 us
    ppermute x1, waiting for transfers between devices, extended(): after = lax.ppermute(first, axis, down)  3.58 us
    sub x1, other arithmetic, block_partial(): scores - row_max[..., None]  2.4 us
  transfers between devices with their start and end apart: 4, of which 4 were waited for; matrix products, arithmetic and copies ran while one was open for 4% of the time, Pallas kernels for 0%

commit v1 on v0

v1 whole, which is shorter than its diff:
```python
import functools
import math

import jax
import jax.numpy as jnp
from jax import lax
from jax.experimental import pallas as pl
from jax.experimental.pallas import tpu as pltpu
from jax.sharding import PartitionSpec as P

HD = 128
NEG_BIG = -1e30
CHUNK = 256
LAG_MP = 4
LAG_SPAN = 10


def fused(
    sections, spans, mps, chunk, lag_mp, lag_span,
    level_ref, window_ref, q_hbm, kv_hbm, lat_hbm, w_hbm, gate_hbm, out_hbm,
    q_buf, kv_buf, lat_buf, w_buf, gate_buf, below, above, att, keep,
    send_mp, recv_mp, send_span, recv_span, send_next,
    load_sems, up_send, up_recv, down_send, down_recv,
    mp_send, mp_recv, span_send, span_recv, next_send, next_recv, relay,
):
    s = lax.axis_index("section")
    x = lax.axis_index("span")
    m = lax.axis_index("mp")
    last = sections - 1
    heads = below.shape[0]
    tokens = kv_buf.shape[1]
    width = kv_buf.shape[2]
    rows = lat_buf.shape[0]
    chunks = keep.shape[0]
    succ = lax.rem(s + 1, sections)
    pred = lax.rem(s + sections - 1, sections)

    barrier = pltpu.get_barrier_semaphore()

    @pl.when(s < last)
    def _():
        pl.semaphore_signal(barrier, 1, device_id={"section": succ})

    @pl.when(s > 0)
    def _():
        pl.semaphore_signal(barrier, 1, device_id={"section": pred})

    for j in range(1, mps):
        pl.semaphore_signal(barrier, 1, device_id={"mp": lax.rem(m + j, mps)})
    for i in range(1, spans):
        pl.semaphore_signal(barrier, 1, device_id={"span": lax.rem(x + i, spans)})
    others = mps - 1 + spans - 1

    loads = [
        pltpu.make_async_copy(q_hbm.at[0], q_buf, load_sems.at[0]),
        pltpu.make_async_copy(kv_hbm.at[:, 0], kv_buf, load_sems.at[1]),
        pltpu.make_async_copy(lat_hbm.at[0], lat_buf, load_sems.at[2]),
        pltpu.make_async_copy(gate_hbm, gate_buf, load_sems.at[3]),
        pltpu.make_async_copy(w_hbm, w_buf, load_sems.at[4]),
    ]

    @pl.when((s > 0) & (s < last))
    def _():
        pl.semaphore_wait(barrier, others + 2)

    @pl.when((s == 0) | (s == last))
    def _():
        pl.semaphore_wait(barrier, others + 1)

    def head_cols(h):
        return pl.ds(pl.multiple_of(h * HD, HD), HD)

    def chunk_cols(c):
        return pl.ds(pl.multiple_of(c * chunk, chunk), chunk)

    def up(h):
        return pltpu.make_async_remote_copy(
            kv_hbm.at[:, 0, :, head_cols(h)], below.at[h], up_send.at[h], up_recv.at[h],
            device_id={"section": succ},
        )

    def down(h):
        return pltpu.make_async_remote_copy(
            kv_hbm.at[:, 0, :, head_cols(h)], above.at[h], down_send.at[h], down_recv.at[h],
            device_id={"section": pred},
        )

    @pl.loop(0, heads)
    def _(h):
        @pl.when(s < last)
        def _():
            up(h).start()

        @pl.when(s > 0)
        def _():
            down(h).start()

    for load in loads:
        load.start()

    @pl.when(s == 0)
    def _():
        below[...] = jnp.zeros_like(below)
        pl.semaphore_signal(relay, 1, device_id={"section": succ})

    @pl.when(s == last)
    def _():
        above[...] = jnp.zeros_like(above)

    pairs = window_ref.shape[0]
    w_lo = jnp.where(s > 0, window_ref[jnp.clip(s - 1, 0, pairs - 1)], 0)
    w_hi = jnp.where(s < last, window_ref[jnp.clip(s, 0, pairs - 1)], 0)
    key_ids = lax.broadcasted_iota(jnp.int32, (1, tokens), 1)
    mask_lo = key_ids >= tokens - w_lo
    mask_hi = key_ids < w_hi
    scale = 1.0 / math.sqrt(HD)
    loads[0].wait()
    loads[1].wait()

    def score(q, k):
        return lax.dot_general(
            q, k, (((1,), (1,)), ((), ())), preferred_element_type=jnp.float32
        ) * scale

    @pl.loop(0, heads)
    def _(h):
        cols = head_cols(h)

        @pl.when(s > 0)
        def _():
            up(h).wait_recv()

        @pl.when(s < last)
        def _():
            down(h).wait_recv()

        q = q_buf[:, cols]
        s_own = score(q, kv_buf[0, :, cols])
        s_lo = jnp.where(mask_lo, score(q, below[h, 0]), NEG_BIG)
        s_hi = jnp.where(mask_hi, score(q, above[h, 0]), NEG_BIG)
        top = jnp.max(jnp.maximum(jnp.maximum(s_lo, s_hi), s_own), axis=1, keepdims=True)
        p_lo = jnp.exp(s_lo - top)
        p_own = jnp.exp(s_own - top)
        p_hi = jnp.exp(s_hi - top)
        total = jnp.sum(p_lo + p_own + p_hi, axis=1, keepdims=True)
        weighted = (
            jnp.dot(p_own.astype(jnp.bfloat16), kv_buf[1, :, cols], preferred_element_type=jnp.float32)
            + jnp.dot(p_lo.astype(jnp.bfloat16), below[h, 1], preferred_element_type=jnp.float32)
            + jnp.dot(p_hi.astype(jnp.bfloat16), above[h, 1], preferred_element_type=jnp.float32)
        )
        result = (weighted / total).astype(jnp.bfloat16).reshape(spans, mps, rows, HD)
        for xb in range(spans):
            for mb in range(mps):
                att[lax.rem(mb - m + mps, mps), lax.rem(xb - x + spans, spans), :, cols] = result[xb, mb]

    @pl.when((s > 0) & (s < last))
    def _():
        pl.semaphore_wait(relay, 1)
        pl.semaphore_signal(relay, 1, device_id={"section": succ})

    @pl.when(s == last)
    def _():
        pl.semaphore_wait(relay, 1)

    for load in loads[2:]:
        load.wait()
    level = level_ref[0]

    def to_mp(j, c):
        return pltpu.make_async_remote_copy(
            send_mp.at[j - 1, c], recv_mp.at[j - 1, c], mp_send.at[j - 1, c], mp_recv.at[j - 1, c],
            device_id={"mp": lax.rem(m + j, mps)},
        )

    def to_span(i, c):
        return pltpu.make_async_remote_copy(
            send_span.at[i - 1, c], recv_span.at[i - 1, c],
            span_send.at[i - 1, c], span_recv.at[i - 1, c],
            device_id={"span": lax.rem(x + i, spans)},
        )

    def to_next(c):
        return pltpu.make_async_remote_copy(
            send_next.at[c], out_hbm.at[0, :, chunk_cols(c)], next_send.at[c], next_recv.at[c],
            device_id={"section": succ},
        )

    def project(c):
        part = jnp.dot(
            att[...].reshape(tokens, width), w_buf[:, chunk_cols(c)],
            preferred_element_type=jnp.float32,
        ).reshape(mps, spans, rows, chunk)
        for j in range(1, mps):
            send_mp[j - 1, c] = part[j].astype(jnp.bfloat16)
            to_mp(j, c).start()
        keep[c] = part[0]

    def reduce_mp(c):
        total = keep[c]
        for j in range(1, mps):
            to_mp(j, c).wait_recv()
            total = total + recv_mp[j - 1, c].astype(jnp.float32)
        for i in range(1, spans):
            send_span[i - 1, c] = total[i].astype(jnp.bfloat16)
            to_span(i, c).start()
        keep[c, 0] = total[0]

    def finish(c):
        total = keep[c, 0]
        for i in range(1, spans):
            to_span(i, c).wait_recv()
            total = total + recv_span[i - 1, c].astype(jnp.float32)
        table = gate_buf[:, chunk_cols(c)]
        level_ids = lax.broadcasted_iota(jnp.int32, table.shape, 0)
        gate = jnp.sum(jnp.where(level_ids == level, table, 0.0), axis=0, keepdims=True)
        updated = lat_buf[:, chunk_cols(c)].astype(jnp.float32) + gate * total
        send_next[c] = updated.astype(jnp.bfloat16)
        to_next(c).start()

    @pl.loop(0, chunks + lag_span)
    def _(step):
        @pl.when(step < chunks)
        def _():
            project(step)

        @pl.when((step >= lag_mp) & (step < chunks + lag_mp))
        def _():
            reduce_mp(step - lag_mp)

        @pl.when(step >= lag_span)
        def _():
            finish(step - lag_span)

    @pl.loop(0, heads)
    def _(h):
        @pl.when(s < last)
        def _():
            up(h).wait_send()

        @pl.when(s > 0)
        def _():
            down(h).wait_send()

    @pl.loop(0, chunks)
    def _(c):
        for j in range(1, mps):
            to_mp(j, c).wait_send()
        for i in range(1, spans):
            to_span(i, c).wait_send()
        to_next(c).wait()


def shards(sizes, queries, keys_values, latents, out_weight, gate_table, level_index, pair_window):
    sections, spans, mps = sizes
    tokens, width = queries.shape[1:]
    rows, model = latents.shape[1:]
    heads = width // HD
    chunk = CHUNK if model % CHUNK == 0 else HD
    chunks = model // chunk
    bf16, f32 = jnp.bfloat16, jnp.float32
    dma = pltpu.SemaphoreType.DMA
    hbm = pl.BlockSpec(memory_space=pltpu.HBM)
    smem = pl.BlockSpec(memory_space=pltpu.SMEM)
    return pl.pallas_call(
        functools.partial(fused, sections, spans, mps, chunk, LAG_MP, LAG_SPAN),
        out_shape=jax.ShapeDtypeStruct(latents.shape, bf16),
        in_specs=[smem, smem, hbm, hbm, hbm, hbm, hbm],
        out_specs=hbm,
        scratch_shapes=[
            pltpu.VMEM((tokens, width), bf16),
            pltpu.VMEM((2, tokens, width), bf16),
            pltpu.VMEM((rows, model), bf16),
            pltpu.VMEM(out_weight.shape, bf16),
            pltpu.VMEM(gate_table.shape, f32),
            pltpu.VMEM((heads, 2, tokens, HD), bf16),
            pltpu.VMEM((heads, 2, tokens, HD), bf16),
            pltpu.VMEM((mps, spans, rows, width), bf16),
            pltpu.VMEM((chunks, spans, rows, chunk), f32),
            pltpu.VMEM((mps - 1, chunks, spans, rows, chunk), bf16),
            pltpu.VMEM((mps - 1, chunks, spans, rows, chunk), bf16),
            pltpu.VMEM((spans - 1, chunks, rows, chunk), bf16),
            pltpu.VMEM((spans - 1, chunks, rows, chunk), bf16),
            pltpu.VMEM((chunks, rows, chunk), bf16),
            dma((5,)),
            dma((heads,)), dma((heads,)), dma((heads,)), dma((heads,)),
            dma((mps - 1, chunks)), dma((mps - 1, chunks)),
            dma((spans - 1, chunks)), dma((spans - 1, chunks)),
            dma((chunks,)), dma((chunks,)),
            pltpu.SemaphoreType.REGULAR,
        ],
        compiler_params=pltpu.CompilerParams(
            collective_id=0, has_side_effects=True, vmem_limit_bytes=60 * 1024 * 1024
        ),
    )(level_index, pair_window, queries, keys_values, latents, out_weight, gate_table)


def solution(mesh):
    sizes = (mesh.shape["section"], mesh.shape["span"], mesh.shape["mp"])
    in_specs = (
        P(("group", "section"), None, ("span", "mp")),
        P(None, ("group", "section"), None, ("span", "mp")),
        P(("group", "section"), ("span", "mp"), None),
        P(("span", "mp"), None),
        P(),
        P(("group", "section")),
        P("group"),
    )
    out_specs = P(("group", "section"), ("span", "mp"), None)
    return jax.shard_map(
        functools.partial(shards, sizes), mesh=mesh, in_specs=in_specs, out_specs=out_specs,
        check_vma=False,
    )
```

time: 111 us -> 57.9 us (0.52)
  waiting for transfers between devices: 69.9 us -> 0 us
  Pallas kernels: 0 us -> 55.1 us
  between operations: 15.5 us -> 0.66 us
  starting transfers between devices: 8.88 us -> 0 us
  matrix products: 5.96 us -> 0 us
  local copies, waits for them, and re-layouts: 6.43 us -> 1.97 us
  other arithmetic: 3.82 us -> 0 us
    pallas_call x0 -> x1, Pallas kernels: none -> 55.1 us  [shards(): pl.pallas_call(functools.partial(fused, sections, spans, mps, chunk, LAG_...]
    ppermute x3 -> x0, waiting for transfers between devices: 36.8 us -> none  [the longest x1 16.6 us: from_behind(): return lax.ppermute(value, axis, pairs)]
    reduce_scatter x1 -> x0, waiting for transfers between devices: 33.1 us -> none  [shards(): lax.psum_scatter(jnp.dot(attended, out_weight, preferred_element_type=jnp...]
    ppermute x3 -> x0, starting transfers between devices: 8.88 us -> none  [the longest x1 6.05 us: extended(): before = lax.ppermute(last, axis, up)]
    dot_general x3 -> x0, matrix products: 5.96 us -> none  [the longest x1 4.28 us: shards(): jnp.dot(attended, out_weight, preferred_element_type=jnp.float32)]
    unnamed x18 -> x1, local copies, waits for them, and re-layouts: 4.4 us -> 1.97 us
    sub x1 -> x0, other arithmetic: 2.4 us -> none  [block_partial(): scores - row_max[..., None]]
    dynamic_slice x1 -> x0, local copies, waits for them, and re-layouts: 1.39 us -> none  [shards(): pair_window[jnp.clip(section_id - 1, 0, final_pair)]]
  transfers between devices with their start and end apart: 4 -> 0, of which waited for: 4 -> 0; matrix products, arithmetic and copies ran while one was open for 4% -> 0% of each run, Pallas kernels for 0% -> 0%
where the time goes in v1:
time: 57.9 us; the launch traced here: 57.7 us
  Pallas kernels  55.1 us (95%)
  local copies, waits for them, and re-layouts  1.97 us (3%)
  between operations  0.66 us (1%)
    pallas_call x1, Pallas kernels, shards(): pl.pallas_call(functools.partial(fused, sections, spans, mps, chunk, LAG_...  55.1 us
    unnamed x1, local copies, waits for them, and re-layouts  1.97 us

profile of v1, /device:TPU:0, one launch (start us, length us, event | category | flops | bytes accessed | tf_op | source)
XLA Modules:
  0.0 57.7 jit_solution(3481316199776448814)
XLA Ops:
  0.7 55.1 %shard_map.73 = bf16[1,64,5120]{2,1,0:T(8,128)(2,1)} custom-call(s32[1]{0:T(128)S(6)} %copy.9.level_ref, s32[3]{0:T(128)} %window_ref.1, bf16[1,256,1024]{2,1,0:T(8,128)(2,1)} %q_hbm.1, bf16[2,1,256,1024]{3,2,1,0:T(8,128)(2,1)} %kv_hbm.1, bf16[1,64,5120]{2,1,0:T(8,128)(2,1)} %lat_hbm.1, bf16[1024,5120]{1,0:T(8,128)(2,1)} %w_hbm.1, f32[8,5120]{1,0:T(8,128)} %gate_hbm.1), custom_call_target="tpu_custom_call" | custom-call | tf_op jit(solution)/shard_map/pallas_call | solution.py:264
  55.8 2.0 %copy.10 = bf16[1,64,5120]{2,1,0:T(8,128)(2,1)} copy(bf16[1,64,5120]{2,1,0:T(8,128)(2,1)} %shard_map.73) | data formatting | bytes 1310720

commit v2 on v1

--- a/solution.py
+++ b/solution.py
@@ -11,16 +11,16 @@
 HD = 128
 NEG_BIG = -1e30
 CHUNK = 256
-LAG_MP = 4
-LAG_SPAN = 10
+LAG_MP = 3
+LAG_SPAN = 8
 
 
 def fused(
     sections, spans, mps, chunk, lag_mp, lag_span,
-    level_ref, window_ref, q_hbm, kv_hbm, lat_hbm, w_hbm, gate_hbm, out_hbm,
+    level_hbm, window_hbm, q_hbm, kv_hbm, lat_hbm, w_hbm, gate_hbm, out_hbm,
     q_buf, kv_buf, lat_buf, w_buf, gate_buf, below, above, att, keep,
     send_mp, recv_mp, send_span, recv_span, send_next,
-    load_sems, up_send, up_recv, down_send, down_recv,
+    level_ref, window_ref, load_sems, up_send, up_recv, down_send, down_recv,
     mp_send, mp_recv, span_send, span_recv, next_send, next_recv, relay,
 ):
     s = lax.axis_index("section")
@@ -51,12 +51,14 @@
         pl.semaphore_signal(barrier, 1, device_id={"span": lax.rem(x + i, spans)})
     others = mps - 1 + spans - 1
 
+    windows = pltpu.make_async_copy(window_hbm, window_ref, load_sems.at[6])
     loads = [
         pltpu.make_async_copy(q_hbm.at[0], q_buf, load_sems.at[0]),
         pltpu.make_async_copy(kv_hbm.at[:, 0], kv_buf, load_sems.at[1]),
         pltpu.make_async_copy(lat_hbm.at[0], lat_buf, load_sems.at[2]),
         pltpu.make_async_copy(gate_hbm, gate_buf, load_sems.at[3]),
         pltpu.make_async_copy(w_hbm, w_buf, load_sems.at[4]),
+        pltpu.make_async_copy(level_hbm, level_ref, load_sems.at[5]),
     ]
 
     @pl.when((s > 0) & (s < last))
@@ -95,6 +97,7 @@
         def _():
             down(h).start()
 
+    windows.start()
     for load in loads:
         load.start()
 
@@ -107,6 +110,7 @@
     def _():
         above[...] = jnp.zeros_like(above)
 
+    windows.wait()
     pairs = window_ref.shape[0]
     w_lo = jnp.where(s > 0, window_ref[jnp.clip(s - 1, 0, pairs - 1)], 0)
     w_hi = jnp.where(s < last, window_ref[jnp.clip(s, 0, pairs - 1)], 0)
@@ -260,11 +264,10 @@
     bf16, f32 = jnp.bfloat16, jnp.float32
     dma = pltpu.SemaphoreType.DMA
     hbm = pl.BlockSpec(memory_space=pltpu.HBM)
-    smem = pl.BlockSpec(memory_space=pltpu.SMEM)
     return pl.pallas_call(
         functools.partial(fused, sections, spans, mps, chunk, LAG_MP, LAG_SPAN),
         out_shape=jax.ShapeDtypeStruct(latents.shape, bf16),
-        in_specs=[smem, smem, hbm, hbm, hbm, hbm, hbm],
+        in_specs=[hbm, hbm, hbm, hbm, hbm, hbm, hbm],
         out_specs=hbm,
         scratch_shapes=[
             pltpu.VMEM((tokens, width), bf16),
@@ -281,7 +284,9 @@
             pltpu.VMEM((spans - 1, chunks, rows, chunk), bf16),
             pltpu.VMEM((spans - 1, chunks, rows, chunk), bf16),
             pltpu.VMEM((chunks, rows, chunk), bf16),
-            dma((5,)),
+            pltpu.SMEM(level_index.shape, jnp.int32),
+            pltpu.SMEM(pair_window.shape, jnp.int32),
+            dma((7,)),
             dma((heads,)), dma((heads,)), dma((heads,)), dma((heads,)),
             dma((mps - 1, chunks)), dma((mps - 1, chunks)),
             dma((spans - 1, chunks)), dma((spans - 1, chunks)),

time: 57.9 us -> 57.2 us (0.988)
  Pallas kernels: 55.1 us -> 54.5 us
    pallas_call x1, Pallas kernels: 55.1 us -> 54.5 us  [shards(): pl.pallas_call(functools.partial(fused, sections, spans, mps, chunk, LAG_...]
where the time goes in v2:
time: 57.2 us; the launch traced here: 57.1 us
  Pallas kernels  54.5 us (95%)
  local copies, waits for them, and re-layouts  1.97 us (3%)
  between operations  0.66 us (1%)
    pallas_call x1, Pallas kernels, shards(): pl.pallas_call(functools.partial(fused, sections, spans, mps, chunk, LAG_...  54.5 us
    unnamed x1, local copies, waits for them, and re-layouts  1.97 us

profile of v2, /device:TPU:0, one launch (start us, length us, event | category | flops | bytes accessed | tf_op | source)
XLA Modules:
  0.0 57.1 jit_solution(6807430454273014579)
XLA Ops:
  0.7 54.5 %shard_map.73 = bf16[1,64,5120]{2,1,0:T(8,128)(2,1)} custom-call(s32[1]{0:T(128)S(6)} %copy.9.level_hbm, s32[3]{0:T(128)} %window_hbm.1, bf16[1,256,1024]{2,1,0:T(8,128)(2,1)} %q_hbm.1, bf16[2,1,256,1024]{3,2,1,0:T(8,128)(2,1)} %kv_hbm.1, bf16[1,64,5120]{2,1,0:T(8,128)(2,1)} %lat_hbm.1, bf16[1024,5120]{1,0:T(8,128)(2,1)} %w_hbm.1, f32[8,5120]{1,0:T(8,128)} %gate_hbm.1), custom_call_target="tpu_custom_call" | custom-call | tf_op jit(solution)/shard_map/pallas_call | solution.py:267
  55.1 2.0 %copy.10 = bf16[1,64,5120]{2,1,0:T(8,128)(2,1)} copy(bf16[1,64,5120]{2,1,0:T(8,128)(2,1)} %shard_map.73) | data formatting | bytes 1310720

commit v3 on v2

--- a/solution.py
+++ b/solution.py
@@ -93,6 +93,8 @@
         def _():
             up(h).start()
 
+    @pl.loop(0, heads)
+    def _(h):
         @pl.when(s > 0)
         def _():
             down(h).start()
@@ -129,17 +131,17 @@
     @pl.loop(0, heads)
     def _(h):
         cols = head_cols(h)
-
-        @pl.when(s > 0)
-        def _():
-            up(h).wait_recv()
-
-        @pl.when(s < last)
-        def _():
-            down(h).wait_recv()
-
         q = q_buf[:, cols]
         s_own = score(q, kv_buf[0, :, cols])
+
+        @pl.when(s > 0)
+        def _():
+            up(h).wait_recv()
+
+        @pl.when(s < last)
+        def _():
+            down(h).wait_recv()
+
         s_lo = jnp.where(mask_lo, score(q, below[h, 0]), NEG_BIG)
         s_hi = jnp.where(mask_hi, score(q, above[h, 0]), NEG_BIG)
         top = jnp.max(jnp.maximum(jnp.maximum(s_lo, s_hi), s_own), axis=1, keepdims=True)

time: 57.2 us -> 57.2 us (level)
  no operation moved by 1% of the time
where the time goes in v3:
time: 57.2 us; the launch traced here: 57 us
  Pallas kernels  54.4 us (95%)
  local copies, waits for them, and re-layouts  1.97 us (3%)
  between operations  0.66 us (1%)
    pallas_call x1, Pallas kernels, shards(): pl.pallas_call(functools.partial(fused, sections, spans, mps, chunk, LAG_...  54.4 us
    unnamed x1, local copies, waits for them, and re-layouts  1.97 us

profile of v3, /device:TPU:0, one launch (start us, length us, event | category | flops | bytes accessed | tf_op | source)
XLA Modules:
  0.0 57.0 jit_solution(17587176295551845929)
XLA Ops:
  0.7 54.4 %shard_map.73 = bf16[1,64,5120]{2,1,0:T(8,128)(2,1)} custom-call(s32[1]{0:T(128)S(6)} %copy.9.level_hbm, s32[3]{0:T(128)} %window_hbm.1, bf16[1,256,1024]{2,1,0:T(8,128)(2,1)} %q_hbm.1, bf16[2,1,256,1024]{3,2,1,0:T(8,128)(2,1)} %kv_hbm.1, bf16[1,64,5120]{2,1,0:T(8,128)(2,1)} %lat_hbm.1, bf16[1024,5120]{1,0:T(8,128)(2,1)} %w_hbm.1, f32[8,5120]{1,0:T(8,128)} %gate_hbm.1), custom_call_target="tpu_custom_call" | custom-call | tf_op jit(solution)/shard_map/pallas_call | solution.py:269
  55.0 2.0 %copy.10 = bf16[1,64,5120]{2,1,0:T(8,128)(2,1)} copy(bf16[1,64,5120]{2,1,0:T(8,128)(2,1)} %shard_map.73) | data formatting | bytes 1310720
